TPU v7x, 256 devices: a whole 4x4x8 slice. The times are simulated.
256 devices in a mesh: row: 8 (over y, core), col: 32 (over z, x).
Axes of the slice: x: 4, y: 4, z: 8, core: 2. Of those that a mesh axis runs over, the one named last changes fastest.
Arguments:
- solution: float32 [8, 32, 16, 128, 128], P('row', 'col'), may hold values from -6 to 6
- residual: float32 [8, 32, 16, 128, 128], P('row', 'col'), may hold values from -6 to 6, as said below
- prev_direction: float32 [8, 32, 16, 128, 128], P('row', 'col'), may hold values from -6 to 6, as said below
- prev_dot: float32 [128], replicated, may hold values from 262144 to 1048576
- face_lists: int32 [8, 32, 4, 4], P('row', 'col'), may hold values from 0 to 16, as said below
- multiplicity: int32 [8, 32, 16], P('row', 'col'), may hold values from 1 to 2, as said below
- block_pattern: int32 [8, 32, 16, 3], P('row', 'col'), may hold values from 0 to 15, as said below
- schur: float32 [8, 32, 16, 3, 128, 128], P('row', 'col'), may hold values from -1 to 4, as said below
- neumann_inverse: float32 [8, 32, 16, 3, 128, 128], P('row', 'col'), may hold values from 0 to 2, as said below
- coarse_basis: float32 [8, 32, 8, 2048], P('row', 'col'), may hold values from -0.25 to 0.25
- primal_map: int32 [8, 32, 8], P('row', 'col'), may hold values from 0 to 1023, all different within a row
- coarse_inverse: float32 [1024, 1024], P('col'), may hold values from -1 to 1, as said below
Outputs:
- new_solution: float32 [8, 32, 16, 128, 128], P('row', 'col')
- new_residual: float32 [8, 32, 16, 128, 128], P('row', 'col')
- direction: float32 [8, 32, 16, 128, 128], P('row', 'col')
Inputs may be any that keep to these rules, and one draw needn't show every extreme that they name: face_lists[i, j, f, k] names the interface blocks that subdomain (i, j) shares with its neighbour across face f (0 toward row i-1, 1 toward row i+1, 2 toward column j-1, 3 toward column j+1); slot k of a face names the same unknowns as slot k of the neighbour's list for the facing face, and both lists have the same length, 1 to 4 blocks, none on faces at the grid's edge; unused slots hold 16; no block lies on two faces; some face holds 4 blocks. multiplicity is 2 for blocks named in face_lists and 1 for the others. block_pattern[i, j, b, 0] = b; the two other entries of block row b are two other blocks, each of which lists b in turn. `schur`: each subdomain's Schur complement is symmetric positive definite, with positive diagonal and no positive entry off it. `neumann_inverse`: each subdomain's local solve matrix is symmetric positive definite. `coarse_inverse`: symmetric positive definite. `residual`: copies of an unknown held by two subdomains (slot k of facing lists) are equal. `prev_direction`: copies of an unknown held by two subdomains (slot k of facing lists) are equal.
All inputs are finite; a program needn't handle non-finite values.
Results may differ from a plain program's by a relative error of at most 0.0003.
Values sent between devices are 32-bit elements; how exact they have to be, the bound alone decides.
A program may use at most 128 MiB of HBM per device.

v0:
```python
import jax
import jax.numpy as jnp
from jax import lax
from jax.sharding import PartitionSpec as P

HIGH = lax.Precision.HIGHEST


def extended(cells, sides, width):
    for axis, dim in sides:
        count = lax.axis_size(axis)
        ends = count - 1
        head = lax.slice_in_dim(cells, 0, width, axis=dim)
        tail = lax.slice_in_dim(cells, cells.shape[dim] - width, cells.shape[dim], axis=dim)
        cells = jnp.concatenate(
            [
                lax.ppermute(tail, axis, [(i, (i + 1) % count) for i in range(ends)]),
                cells,
                lax.ppermute(head, axis, [((i + 1) % count, i) for i in range(ends)]),
            ],
            axis=dim,
        )
    return cells


def block_product(blocks, pattern, values_in):
    stacked_count, block_count, dofs, cases = values_in.shape
    gathered = jnp.take(values_in, pattern.reshape(-1), axis=1)
    gathered = gathered.reshape(stacked_count, block_count, pattern.shape[1], dofs, cases)
    return jnp.einsum("bkij,vbkjn->vbin", blocks, gathered, precision=HIGH)


def assemble(values_in, faces):
    stacked_count, block_count, dofs, cases = values_in.shape
    flattened = values_in.reshape(stacked_count, block_count, dofs * cases)
    indicator = (faces[..., None] == jnp.arange(block_count)).astype(jnp.float32)
    face_values = jnp.einsum("fkb,vbc->fvkc", indicator, flattened, precision=HIGH)
    row_faces = extended(face_values[0:2], (("row", 0),), 1)
    col_faces = extended(face_values[2:4], (("col", 0),), 1)
    received = jnp.stack([row_faces[0], row_faces[3], col_faces[0], col_faces[3]])
    added = jnp.einsum("fkb,fvkc->vbc", indicator, received, precision=HIGH)
    return (flattened + added).reshape(values_in.shape)


def precondition(residual, weight, faces, pattern, neumann, basis, primal_map, inverse_rows):
    scaled = residual * weight
    local_term = block_product(neumann, pattern, scaled[None])[0]
    cases = residual.shape[-1]
    coarse_local = jnp.dot(basis, scaled.reshape(-1, cases), precision=HIGH)
    owned_count, coarse_total_rows = inverse_rows.shape
    indicator = (primal_map[:, None] == jnp.arange(coarse_total_rows)).astype(jnp.float32)
    owned_rhs = lax.psum_scatter(
        jnp.dot(indicator.T, coarse_local, precision=HIGH), "col", scatter_dimension=0, tiled=True
    )
    owned_rhs = lax.psum(owned_rhs, "row")
    columns = inverse_rows
    owned_solution = jnp.dot(
        columns, lax.all_gather(owned_rhs, "col", axis=0, tiled=True), precision=HIGH
    )
    columns = indicator
    own_coarse = jnp.dot(
        columns, lax.all_gather(owned_solution, "col", axis=0, tiled=True), precision=HIGH
    )
    coarse_back = jnp.dot(basis.T, own_coarse, precision=HIGH).reshape(residual.shape)
    return assemble(((local_term + coarse_back) * weight)[None], faces)[0]


def per_device(
    solution,
    residual,
    prev_direction,
    prev_dot,
    face_lists,
    multiplicity,
    block_pattern,
    schur,
    neumann_inverse,
    coarse_basis,
    primal_map,
    coarse_inverse,
):
    faces = face_lists[0, 0]
    pattern = block_pattern[0, 0]
    weight = (1.0 / multiplicity[0, 0].astype(jnp.float32))[:, None, None]
    current = residual[0, 0]
    previous = prev_direction[0, 0]
    precond = precondition(
        current,
        weight,
        faces,
        pattern,
        neumann_inverse[0, 0],
        coarse_basis[0, 0],
        primal_map[0, 0],
        coarse_inverse,
    )
    local_precond_dot = jnp.sum(current * precond * weight, axis=(0, 1))
    precond_dot = lax.psum(local_precond_dot, ("row", "col"))
    direction_mix = precond_dot / prev_dot
    direction = precond + direction_mix * previous
    image = assemble(block_product(schur[0, 0], pattern, direction[None]), faces)[0]
    curvature = lax.psum(jnp.sum(direction * image * weight, axis=(0, 1)), ("row", "col"))
    step_size = precond_dot / curvature
    new_solution = solution[0, 0] + step_size * direction
    new_residual = current - step_size * image
    return (new_solution[None, None], new_residual[None, None], direction[None, None])


def solution(mesh):
    placed = (
        P("row", "col", None, None, None),
        P("row", "col", None, None, None),
        P("row", "col", None, None, None),
        P(),
        P("row", "col", None, None),
        P("row", "col", None),
        P("row", "col", None, None),
        P("row", "col", None, None, None, None),
        P("row", "col", None, None, None, None),
        P("row", "col", None, None),
        P("row", "col", None),
        P("col", None),
    )
    return jax.shard_map(
        per_device,
        mesh=mesh,
        in_specs=placed,
        out_specs=(
            P("row", "col", None, None, None),
            P("row", "col", None, None, None),
            P("row", "col", None, None, None),
        ),
        check_vma=False,
    )
```

profile of v0, /device:TPU:1, one launch (start us, length us, event | category | flops | bytes accessed | tf_op | source)
XLA Modules:
  0.0 597.9 jit_solution(11276702184320067996)
XLA Ops:
  12.5 2.3 fusion.31
  15.1 3.6 gather_fusion
  20.9 6.2 %fusion.6 = f32[1,16,128,128]{2,3,1,0:T(8,128)} fusion(f32[16,3,128,128]{3,2,1,0:T(8,128)S(1)} %bitcast.147, f32[1,1,16,3,128,128]{5,4,3,2,1,0:T(8,128)S(1)} %copy-done), kind=kOutput, calls=%fused_computation.15 | convolution fusion | flops 1207959552 | bytes 7340032 | tf_op jit(solution)/shard_map/bkij,vbkjn->vbin/dot_general | solution.py:30
  27.1 2.6 copy.44
  29.7 194.6 %reduce-scatter.2.cloned.1.call-done = f32[32,128]{1,0:T(8,128)} async-done(((f32[1024,128]{1,0:T(8,128)}), f32[32,128]{1,0:T(8,128)}) %reduce-scatter.2.cloned.1.call-update) | async-done | bytes 16400 | tf_op jit(solution)/shard_map/reduce_scatter | solution.py:52
  224.3 26.4 %psum.21 = f32[32,128]{1,0:T(8,128)S(1)} all-reduce(f32[32,128]{1,0:T(8,128)} %reduce-scatter.2.cloned.1.call-done), channel_id=1, replica_groups=mesh['row'=8,'col'=32] {'row'}, use_global_device_ids=true, to_apply=%region_1.3 | all-reduce | flops 4096 | bytes 32768 | tf_op jit(solution)/shard_map/psum | solution.py:55
  250.7 35.9 %all_gather.6 = f32[1024,128]{1,0:T(8,128)S(1)} all-gather(f32[32,128]{1,0:T(8,128)S(1)} %psum.21), channel_id=1, replica_groups=mesh['row'=8,'col'=32] {'col'}, dimensions={0}, use_global_device_ids=true | all-gather | bytes 540672 | tf_op jit(solution)/shard_map/all_gather | solution.py:58
  287.0 35.8 %all_gather.7 = f32[1024,128]{1,0:T(8,128)S(1)} all-gather(f32[32,128]{1,0:T(8,128)S(1)} %convolution_bitcast_fusion.5), channel_id=1, replica_groups=mesh['row'=8,'col'=32] {'col'}, dimensions={0}, use_global_device_ids=true | all-gather | bytes 540672 | tf_op jit(solution)/shard_map/all_gather | solution.py:62
  325.0 2.5 copy.42
  327.6 2.4 reshape.184
  329.9 3.0 convolution_bitcast_fusion.3
  333.9 27.6 %collective-permute-start = (f32[1,1,4,16384]{3,2,0,1:T(4,128)}, f32[1,1,4,16384]{3,2,0,1:T(4,128)}, u32[]{:S(2)}, u32[]{:S(2)}) collective-permute-start(f32[1,1,4,16384]{3,2,0,1:T(4,128)} %get-tuple-element.10), channel_id=1, source_target_pairs={{0,32},{32,64},{64,96},{96,128},{128,160},{160,192},{192,224},{1,3... | collective-permute-start | bytes 786440 | tf_op jit(solution)/shard_map/ppermute | solution.py:17
  361.5 3.8 collective-permute-start.1
  365.4 3.1 collective-permute-start.2
  369.7 2.5 copy.41
  372.2 2.4 squeeze.32
  374.6 2.4 reshape.183
  378.6 3.4 fusion.1
  384.5 78.4 %psum.22 = f32[128]{0:T(128)S(1)} all-reduce(f32[128]{0:T(128)S(1)} %fusion.14), channel_id=1, replica_groups=mesh['row'=8,'col'=32] {'row','col'}, use_global_device_ids=true, to_apply=%region_3.5 | all-reduce | flops 128 | bytes 1024 | tf_op jit(solution)/shard_map/psum | solution.py:98
  462.9 2.7 fusion.12
  465.5 3.6 gather_fusion.1
  469.1 2.3 bitcast_select_fusion
  472.0 6.3 %fusion.9 = f32[1,16,128,128]{2,3,1,0:T(8,128)} fusion(f32[16,3,128,128]{3,2,1,0:T(8,128)S(1)} %bitcast.146, f32[1,1,16,3,128,128]{5,4,3,2,1,0:T(8,128)S(1)} %copy-done.7), kind=kOutput, calls=%fused_computation.16 | convolution fusion | flops 1207959552 | bytes 7340032 | tf_op jit(solution)/shard_map/bkij,vbkjn->vbin/dot_general | solution.py:30
  478.3 2.5 copy.47
  480.8 2.4 reshape.224
  483.2 2.4 reshape.187
  485.6 2.4 convolution_bitcast_fusion.1
  488.1 3.7 collective-permute-start.4
  497.0 2.5 collective-permute-done.5
  501.7 4.1 collective-permute-done.7
  508.2 78.4 %psum.23 = f32[128]{0:T(128)S(1)} all-reduce(f32[128]{0:T(128)S(1)} %bitcast_reduce_fusion), channel_id=1, replica_groups=mesh['row'=8,'col'=32] {'row','col'}, use_global_device_ids=true, to_apply=%region_6.8 | all-reduce | flops 128 | bytes 1024 | tf_op jit(solution)/shard_map/psum | solution.py:102
  586.6 4.5 multiply_add_fusion
  (63 shorter events, 27.0 us)
Async XLA Ops:
  7.2 13.7 %copy-start = (f32[1,1,16,3,128,128]{5,4,3,2,1,0:T(8,128)S(1)}, f32[1,1,16,3,128,128]{5,4,3,2,1,0:T(8,128)}, u32[]{:S(2)}) copy-start(f32[1,1,16,3,128,128]{5,4,3,2,1,0:T(8,128)} %param.22) | copy-start | bytes 9437188
  7.2 3.8 copy-start.11
  7.2 217.1 %reduce-scatter.2.cloned.1.call-start = ((), (), s32[]{:S(2)}) async-start(), calls=%async_computation.1 | async-start | bytes 540672 | tf_op jit(solution)/shard_map/reduce_scatter | solution.py:52
  8.0 6.8 %copy-start.12 = (s32[1,1,16,3]{2,1,3,0:T(1,128)S(1)}, s32[1,1,16,3]{2,1,3,0:T(1,128)}, u32[]{:S(2)}) copy-start(s32[1,1,16,3]{2,1,3,0:T(1,128)} %param.20) | copy-start | bytes 580
  20.9 265.7 %copy-start.9 = (f32[32,1024]{1,0:T(8,128)S(1)}, f32[32,1024]{1,0:T(8,128)}, u32[]{:S(2)}) copy-start(f32[32,1024]{1,0:T(8,128)} %param.25) | copy-start | bytes 393220
  27.1 295.9 %copy-start.8 = (f32[1,1,8,2048]{3,2,1,0:T(8,128)S(1)}, f32[1,1,8,2048]{3,2,1,0:T(8,128)}, u32[]{:S(2)}) copy-start(f32[1,1,8,2048]{3,2,1,0:T(8,128)} %param.23) | copy-start | bytes 196612
  286.9 43.0 %copy-start.10 = (s32[1,1,4,4]{3,2,1,0:T(4,128)S(1)}, s32[1,1,4,4]{3,2,1,0:T(4,128)}, u32[]{:S(2)}) copy-start(s32[1,1,4,4]{3,2,1,0:T(4,128)} %param.18) | copy-start | bytes 196
  333.9 43.1 %collective-permute-start = (f32[1,1,4,16384]{3,2,0,1:T(4,128)}, f32[1,1,4,16384]{3,2,0,1:T(4,128)}, u32[]{:S(2)}, u32[]{:S(2)}) collective-permute-start(f32[1,1,4,16384]{3,2,0,1:T(4,128)} %get-tuple-element.10), channel_id=1, source_target_pairs={{0,32},{32,64},{64,96},{96,128},{128,160},{160,192},{192,224},{1,3... | collective-permute-start | bytes 786440 | tf_op jit(solution)/shard_map/ppermute | solution.py:17
  361.5 15.5 %collective-permute-start.1 = (f32[1,1,4,16384]{3,2,0,1:T(4,128)}, f32[1,1,4,16384]{3,2,0,1:T(4,128)}, u32[]{:S(2)}, u32[]{:S(2)}) collective-permute-start(f32[1,1,4,16384]{3,2,0,1:T(4,128)} %get-tuple-element.13), channel_id=1, source_target_pairs={{32,0},{64,32},{96,64},{128,96},{160,128},{192,160},{224,192},{33,... | collective-permute-start | bytes 786440 | tf_op jit(solution)/shard_map/ppermute | solution.py:19
  365.4 11.7 %collective-permute-start.2 = (f32[1,1,4,16384]{3,2,0,1:T(4,128)}, f32[1,1,4,16384]{3,2,0,1:T(4,128)}, u32[]{:S(2)}, u32[]{:S(2)}) collective-permute-start(f32[1,1,4,16384]{3,2,0,1:T(4,128)} %get-tuple-element.12), channel_id=1, source_target_pairs={{0,1},{1,2},{2,3},{3,4},{4,5},{5,6},{6,7},{7,8},{8,9},{9,10},{10,1... | collective-permute-start | bytes 786440 | tf_op jit(solution)/shard_map/ppermute | solution.py:17
  368.4 10.2 %collective-permute-start.3 = (f32[1,1,4,16384]{3,2,0,1:T(4,128)S(1)}, f32[1,1,4,16384]{3,2,0,1:T(4,128)}, u32[]{:S(2)}, u32[]{:S(2)}) collective-permute-start(f32[1,1,4,16384]{3,2,0,1:T(4,128)S(1)} %get-tuple-element.11), channel_id=1, source_target_pairs={{1,0},{2,1},{3,2},{4,3},{5,4},{6,5},{7,6},{8,7},{9,8},{10,9},{11,1... | collective-permute-start | bytes 786440 | tf_op jit(solution)/shard_map/ppermute | solution.py:19
  378.6 5.5 copy-start.1
  382.0 1.0 copy-start.4
  382.0 80.9 %copy-start.13 = (f32[128]{0:T(128)S(1)}, f32[128]{0:T(128)}, u32[]{:S(2)}) copy-start(f32[128]{0:T(128)} %param.17) | copy-start | bytes 1540
  383.2 1.0 copy-start.2
  469.1 2.8 copy-start.7
  485.6 20.1 %copy-start.3 = (f32[1,16,16384]{2,1,0:T(8,128)S(1)}, f32[1,16,16384]{2,1,0:T(8,128)}, u32[]{:S(2)}) copy-start(f32[1,16,16384]{2,1,0:T(8,128)} %squeeze.32) | copy-start | bytes 3145732
  485.6 20.1 %copy-start.5 = (f32[1,16,16384]{2,1,0:T(8,128)S(1)}, f32[1,16,16384]{2,1,0:T(8,128)}, u32[]{:S(2)}) copy-start(f32[1,16,16384]{2,1,0:T(8,128)} %copy-done.4) | copy-start | bytes 3145732
  485.6 20.1 %copy-start.6 = (f32[1,16,16384]{2,1,0:T(8,128)S(1)}, f32[1,16,16384]{2,1,0:T(8,128)}, u32[]{:S(2)}) copy-start(f32[1,16,16384]{2,1,0:T(8,128)} %reshape.187) | copy-start | bytes 3145732
  488.1 8.9 %collective-permute-start.4 = (f32[1,1,4,16384]{3,2,0,1:T(4,128)S(1)}, f32[1,1,4,16384]{3,2,0,1:T(4,128)S(1)}, u32[]{:S(2)}, u32[]{:S(2)}) collective-permute-start(f32[1,1,4,16384]{3,2,0,1:T(4,128)S(1)} %get-tuple-element.6), channel_id=1, source_target_pairs={{0,32},{32,64},{64,96},{96,128},{128,160},{160,192},{192,224},{1,3... | collective-permute-start | bytes 786440 | tf_op jit(solution)/shard_map/ppermute | solution.py:17
  491.8 7.7 %collective-permute-start.5 = (f32[1,1,4,16384]{3,2,0,1:T(4,128)S(1)}, f32[1,1,4,16384]{3,2,0,1:T(4,128)S(1)}, u32[]{:S(2)}, u32[]{:S(2)}) collective-permute-start(f32[1,1,4,16384]{3,2,0,1:T(4,128)S(1)} %get-tuple-element.9), channel_id=1, source_target_pairs={{32,0},{64,32},{96,64},{128,96},{160,128},{192,160},{224,192},{33,... | collective-permute-start | bytes 786440 | tf_op jit(solution)/shard_map/ppermute | solution.py:19
  493.7 7.9 %collective-permute-start.6 = (f32[1,1,4,16384]{3,2,0,1:T(4,128)S(1)}, f32[1,1,4,16384]{3,2,0,1:T(4,128)S(1)}, u32[]{:S(2)}, u32[]{:S(2)}) collective-permute-start(f32[1,1,4,16384]{3,2,0,1:T(4,128)S(1)} %get-tuple-element.8), channel_id=1, source_target_pairs={{0,1},{1,2},{2,3},{3,4},{4,5},{5,6},{6,7},{7,8},{8,9},{9,10},{10,1... | collective-permute-start | bytes 786440 | tf_op jit(solution)/shard_map/ppermute | solution.py:17
  495.7 10.1 %collective-permute-start.7 = (f32[1,1,4,16384]{3,2,0,1:T(4,128)S(1)}, f32[1,1,4,16384]{3,2,0,1:T(4,128)S(1)}, u32[]{:S(2)}, u32[]{:S(2)}) collective-permute-start(f32[1,1,4,16384]{3,2,0,1:T(4,128)S(1)} %get-tuple-element.7), channel_id=1, source_target_pairs={{1,0},{2,1},{3,2},{4,3},{5,4},{6,5},{7,6},{8,7},{9,8},{10,9},{11,1... | collective-permute-start | bytes 786440 | tf_op jit(solution)/shard_map/ppermute | solution.py:19
Sparse Core Ops, SparseCore 0:
  12.7 211.5 reduce-scatter.1
where the time goes:
time: 599 us; the launch traced here: 598 us
  blocking collectives  255 us (43%)
  waiting for transfers between devices  205 us (34%)
  starting transfers between devices  44.6 us (7%)
  local copies, waits for them, and re-layouts  34.4 us (6%)
  matrix products  28.1 us (5%)
  other arithmetic  16.6 us (3%)
  between operations  14.3 us (2%)
    reduce_scatter x1, waiting for transfers between devices, precondition(): lax.psum_scatter(jnp.dot(indicator.T, coarse_local, precision=HIGH), 'col...  195 us
    psum x1, blocking collectives, per_device(): lax.psum(jnp.sum(direction * image * weight, axis=(0, 1)), ('row', 'col'))  78.4 us
    psum x1, blocking collectives, per_device(): precond_dot = lax.psum(local_precond_dot, ('row', 'col'))  78.4 us
    ppermute x4, starting transfers between devices, extended(): lax.ppermute(tail, axis, [(i, (i + 1) % count) for i in range(ends)])  36.3 us
    all_gather x1, blocking collectives, precondition(): lax.all_gather(owned_rhs, 'col', axis=0, tiled=True)  35.9 us
    all_gather x1, blocking collectives, precondition(): lax.all_gather(owned_solution, 'col', axis=0, tiled=True)  35.8 us
    psum x1, blocking collectives, precondition(): owned_rhs = lax.psum(owned_rhs, 'row')  26.4 us
    dot_general x2, matrix products, block_product(): return jnp.einsum('bkij,vbkjn->vbin', blocks, gathered, precision=HIGH)  12.5 us
  transfers between devices with their start and end apart: 9, of which 5 were waited for; matrix products, arithmetic and copies ran while one was open for 4% of the time, Pallas kernels for 0%

commit v1 on v0

--- a/solution.py
+++ b/solution.py
@@ -54,9 +54,13 @@
     )
     owned_rhs = lax.psum(owned_rhs, "row")
     columns = inverse_rows
-    owned_solution = jnp.dot(
-        columns, lax.all_gather(owned_rhs, "col", axis=0, tiled=True), precision=HIGH
-    )
+
+    def area_unite(own_rows):
+        parts_out = lax.axis_size("col")
+        built = jnp.concatenate([own_rows] * parts_out, axis=0)
+        return lax.all_to_all(built, axis_name="col", split_axis=0, concat_axis=0, tiled=True)
+
+    owned_solution = jnp.dot(columns, area_unite(owned_rhs), precision=HIGH)
     columns = indicator
     own_coarse = jnp.dot(
         columns, lax.all_gather(owned_solution, "col", axis=0, tiled=True), precision=HIGH

time: 599 us -> 574 us (0.958)
  blocking collectives: 255 us -> 220 us
  waiting for transfers between devices: 205 us -> 218 us
    all_gather x1 -> x0, blocking collectives: 35.9 us -> none  [precondition(): lax.all_gather(owned_rhs, 'col', axis=0, tiled=True)]
    reduce_scatter x1, waiting for transfers between devices: 195 us -> 206 us  [precondition(): lax.psum_scatter(jnp.dot(indicator.T, coarse_local, precision=HIGH), 'col...]
    ppermute x4, starting transfers between devices: 36.3 us -> 26.6 us  [extended(): lax.ppermute(tail, axis, [(i, (i + 1) % count) for i in range(ends)])]
    all_to_all x0 -> x1, starting transfers between devices: none -> 6.74 us  [area_unite(): lax.all_to_all(built, axis_name='col', split_axis=0, concat_axis=0, tiled...]
  transfers between devices with their start and end apart: 9 -> 10, of which waited for: 5 -> 6; matrix products, arithmetic and copies ran while one was open for 4% -> 4% of each run, Pallas kernels for 0% -> 0%
where the time goes in v1:
time: 574 us; the launch traced here: 573 us
  blocking collectives  220 us (38%)
  waiting for transfers between devices  218 us (38%)
  starting transfers between devices  40 us (7%)
  local copies, waits for them, and re-layouts  35.3 us (6%)
  matrix products  29.2 us (5%)
  other arithmetic  16.7 us (3%)
  between operations  14.6 us (3%)
    reduce_scatter x1, waiting for transfers between devices, precondition(): lax.psum_scatter(jnp.dot(indicator.T, coarse_local, precision=HIGH), 'col...  206 us
    psum x1, blocking collectives, per_device(): lax.psum(jnp.sum(direction * image * weight, axis=(0, 1)), ('row', 'col'))  78.4 us
    psum x1, blocking collectives, per_device(): precond_dot = lax.psum(local_precond_dot, ('row', 'col'))  77.9 us
    all_gather x1, blocking collectives, precondition(): lax.all_gather(owned_solution, 'col', axis=0, tiled=True)  37 us
    ppermute x4, starting transfers between devices, extended(): lax.ppermute(tail, axis, [(i, (i + 1) % count) for i in range(ends)])  26.6 us
    psum x1, blocking collectives, precondition(): owned_rhs = lax.psum(owned_rhs, 'row')  26.4 us
    dot_general x2, matrix products, block_product(): return jnp.einsum('bkij,vbkjn->vbin', blocks, gathered, precision=HIGH)  12.5 us
  transfers between devices with their start and end apart: 10, of which 6 were waited for; matrix products, arithmetic and copies ran while one was open for 4% of the time, Pallas kernels for 0%

profile of v1, /device:TPU:1, one launch (start us, length us, event | category | flops | bytes accessed | tf_op | source)
XLA Modules:
  0.0 573.2 jit_solution(7345887871936899259)
XLA Ops:
  12.7 2.3 fusion.31
  15.1 3.6 gather_fusion
  18.7 205.6 %reduce-scatter.2.cloned.1.call-done = f32[32,128]{1,0:T(8,128)} async-done(((f32[1024,128]{1,0:T(8,128)}), f32[32,128]{1,0:T(8,128)}) %reduce-scatter.2.cloned.1.call-update) | async-done | bytes 16400 | tf_op jit(solution)/shard_map/reduce_scatter | solution.py:52
  224.3 26.4 %psum.21 = f32[32,128]{1,0:T(8,128)S(1)} all-reduce(f32[32,128]{1,0:T(8,128)} %reduce-scatter.2.cloned.1.call-done), channel_id=1, replica_groups=mesh['row'=8,'col'=32] {'row'}, use_global_device_ids=true, to_apply=%region_1.3 | all-reduce | flops 4096 | bytes 32768 | tf_op jit(solution)/shard_map/psum | solution.py:55
  251.8 6.7 %all-to-all-start = ((f32[32,32,128]{2,1,0:T(8,128)}), f32[32,32,128]{2,1,0:T(8,128)}, u32[]{:S(2)}, u32[]{:S(2)}) async-start(f32[32,32,128]{2,1,0:T(8,128)} %bitcast.156), calls=%async_computation.1 | async-start | bytes 1048576 | tf_op jit(solution)/shard_map/all_to_all | solution.py:61
  260.7 6.2 %fusion.6 = f32[1,16,128,128]{2,3,1,0:T(8,128)} fusion(f32[16,3,128,128]{3,2,1,0:T(8,128)S(1)} %bitcast.149, f32[1,1,16,3,128,128]{5,4,3,2,1,0:T(8,128)S(1)} %copy-done), kind=kOutput, calls=%fused_computation.15 | convolution fusion | flops 1207959552 | bytes 7340032 | tf_op jit(solution)/shard_map/bkij,vbkjn->vbin/dot_general | solution.py:30
  267.0 2.6 copy.44
  272.9 37.0 %all_gather.3 = f32[1024,128]{1,0:T(8,128)S(1)} all-gather(f32[32,128]{1,0:T(8,128)S(1)} %convolution_bitcast_fusion.5), channel_id=1, replica_groups=mesh['row'=8,'col'=32] {'col'}, dimensions={0}, use_global_device_ids=true | all-gather | bytes 540672 | tf_op jit(solution)/shard_map/all_gather | solution.py:66
  312.2 2.5 copy.42
  314.7 2.4 reshape.186
  317.1 3.0 convolution_bitcast_fusion.3
  321.1 18.9 %collective-permute-start = (f32[1,1,4,16384]{3,2,0,1:T(4,128)}, f32[1,1,4,16384]{3,2,0,1:T(4,128)}, u32[]{:S(2)}, u32[]{:S(2)}) collective-permute-start(f32[1,1,4,16384]{3,2,0,1:T(4,128)} %get-tuple-element.10), channel_id=1, source_target_pairs={{0,32},{32,64},{64,96},{96,128},{128,160},{160,192},{192,224},{1,3... | collective-permute-start | bytes 786440 | tf_op jit(solution)/shard_map/ppermute | solution.py:17
  342.2 2.6 collective-permute-start.2
  346.0 2.5 copy.41
  348.6 2.4 squeeze.32
  350.9 2.4 reshape.185
  354.9 3.4 fusion.1
  360.8 77.9 %psum.22 = f32[128]{0:T(128)S(1)} all-reduce(f32[128]{0:T(128)S(1)} %fusion.14), channel_id=1, replica_groups=mesh['row'=8,'col'=32] {'row','col'}, use_global_device_ids=true, to_apply=%region_3.5 | all-reduce | flops 128 | bytes 1024 | tf_op jit(solution)/shard_map/psum | solution.py:102
  438.8 2.7 fusion.12
  441.4 3.6 gather_fusion.1
  445.0 2.3 bitcast_select_fusion
  447.9 6.3 %fusion.9 = f32[1,16,128,128]{2,3,1,0:T(8,128)} fusion(f32[16,3,128,128]{3,2,1,0:T(8,128)S(1)} %bitcast.148, f32[1,1,16,3,128,128]{5,4,3,2,1,0:T(8,128)S(1)} %copy-done.7), kind=kOutput, calls=%fused_computation.16 | convolution fusion | flops 1207959552 | bytes 7340032 | tf_op jit(solution)/shard_map/bkij,vbkjn->vbin/dot_general | solution.py:30
  454.1 2.5 copy.47
  456.7 2.4 reshape.226
  459.1 2.4 reshape.189
  461.5 2.4 convolution_bitcast_fusion.1
  464.0 3.1 collective-permute-start.4
  472.3 2.5 collective-permute-done.5
  474.8 2.2 collective-permute-done.6
  477.0 4.1 collective-permute-done.7
  483.5 78.4 %psum.23 = f32[128]{0:T(128)S(1)} all-reduce(f32[128]{0:T(128)S(1)} %bitcast_reduce_fusion), channel_id=1, replica_groups=mesh['row'=8,'col'=32] {'row','col'}, use_global_device_ids=true, to_apply=%region_6.8 | all-reduce | flops 128 | bytes 1024 | tf_op jit(solution)/shard_map/psum | solution.py:106
  561.9 4.5 multiply_add_fusion
  (98 shorter events, 30.8 us)
Async XLA Ops:
  7.2 253.6 %copy-start = (f32[1,1,16,3,128,128]{5,4,3,2,1,0:T(8,128)S(1)}, f32[1,1,16,3,128,128]{5,4,3,2,1,0:T(8,128)}, u32[]{:S(2)}) copy-start(f32[1,1,16,3,128,128]{5,4,3,2,1,0:T(8,128)} %param.22) | copy-start | bytes 9437188
  7.2 3.8 copy-start.12
  7.2 5.3 copy-start.13
  7.2 217.1 %reduce-scatter.2.cloned.1.call-start = ((), (), s32[]{:S(2)}) async-start(), calls=%async_computation.2 | async-start | bytes 540672 | tf_op jit(solution)/shard_map/reduce_scatter | solution.py:52
  251.0 0.8 copy-start.8
  251.8 19.6 %all-to-all-start = ((f32[32,32,128]{2,1,0:T(8,128)}), f32[32,32,128]{2,1,0:T(8,128)}, u32[]{:S(2)}, u32[]{:S(2)}) async-start(f32[32,32,128]{2,1,0:T(8,128)} %bitcast.156), calls=%async_computation.1 | async-start | bytes 1048576 | tf_op jit(solution)/shard_map/all_to_all | solution.py:61
  260.7 10.7 %copy-start.10 = (f32[32,1024]{1,0:T(8,128)S(1)}, f32[32,1024]{1,0:T(8,128)}, u32[]{:S(2)}) copy-start(f32[32,1024]{1,0:T(8,128)} %param.25) | copy-start | bytes 393220
  267.0 43.2 %copy-start.9 = (f32[1,1,8,2048]{3,2,1,0:T(8,128)S(1)}, f32[1,1,8,2048]{3,2,1,0:T(8,128)}, u32[]{:S(2)}) copy-start(f32[1,1,8,2048]{3,2,1,0:T(8,128)} %param.23) | copy-start | bytes 196612
  272.9 44.2 %copy-start.11 = (s32[1,1,4,4]{3,2,1,0:T(4,128)S(1)}, s32[1,1,4,4]{3,2,1,0:T(4,128)}, u32[]{:S(2)}) copy-start(s32[1,1,4,4]{3,2,1,0:T(4,128)} %param.18) | copy-start | bytes 196
  321.1 32.2 %collective-permute-start = (f32[1,1,4,16384]{3,2,0,1:T(4,128)}, f32[1,1,4,16384]{3,2,0,1:T(4,128)}, u32[]{:S(2)}, u32[]{:S(2)}) collective-permute-start(f32[1,1,4,16384]{3,2,0,1:T(4,128)} %get-tuple-element.10), channel_id=1, source_target_pairs={{0,32},{32,64},{64,96},{96,128},{128,160},{160,192},{192,224},{1,3... | collective-permute-start | bytes 786440 | tf_op jit(solution)/shard_map/ppermute | solution.py:17
  340.0 13.3 %collective-permute-start.1 = (f32[1,1,4,16384]{3,2,0,1:T(4,128)}, f32[1,1,4,16384]{3,2,0,1:T(4,128)}, u32[]{:S(2)}, u32[]{:S(2)}) collective-permute-start(f32[1,1,4,16384]{3,2,0,1:T(4,128)} %get-tuple-element.13), channel_id=1, source_target_pairs={{32,0},{64,32},{96,64},{128,96},{160,128},{192,160},{224,192},{33,... | collective-permute-start | bytes 786440 | tf_op jit(solution)/shard_map/ppermute | solution.py:19
  342.2 11.2 %collective-permute-start.2 = (f32[1,1,4,16384]{3,2,0,1:T(4,128)}, f32[1,1,4,16384]{3,2,0,1:T(4,128)}, u32[]{:S(2)}, u32[]{:S(2)}) collective-permute-start(f32[1,1,4,16384]{3,2,0,1:T(4,128)} %get-tuple-element.12), channel_id=1, source_target_pairs={{0,1},{1,2},{2,3},{3,4},{4,5},{5,6},{6,7},{7,8},{8,9},{9,10},{10,1... | collective-permute-start | bytes 786440 | tf_op jit(solution)/shard_map/ppermute | solution.py:17
  344.7 10.2 %collective-permute-start.3 = (f32[1,1,4,16384]{3,2,0,1:T(4,128)S(1)}, f32[1,1,4,16384]{3,2,0,1:T(4,128)}, u32[]{:S(2)}, u32[]{:S(2)}) collective-permute-start(f32[1,1,4,16384]{3,2,0,1:T(4,128)S(1)} %get-tuple-element.11), channel_id=1, source_target_pairs={{1,0},{2,1},{3,2},{4,3},{5,4},{6,5},{7,6},{8,7},{9,8},{10,9},{11,1... | collective-permute-start | bytes 786440 | tf_op jit(solution)/shard_map/ppermute | solution.py:19
  354.9 5.5 copy-start.1
  358.3 1.0 copy-start.4
  358.3 80.4 %copy-start.14 = (f32[128]{0:T(128)S(1)}, f32[128]{0:T(128)}, u32[]{:S(2)}) copy-start(f32[128]{0:T(128)} %param.17) | copy-start | bytes 1540
  359.5 1.0 copy-start.2
  445.0 2.8 copy-start.7
  461.5 19.6 %copy-start.3 = (f32[1,16,16384]{2,1,0:T(8,128)S(1)}, f32[1,16,16384]{2,1,0:T(8,128)}, u32[]{:S(2)}) copy-start(f32[1,16,16384]{2,1,0:T(8,128)} %squeeze.32) | copy-start | bytes 3145732
  461.5 19.6 %copy-start.5 = (f32[1,16,16384]{2,1,0:T(8,128)S(1)}, f32[1,16,16384]{2,1,0:T(8,128)}, u32[]{:S(2)}) copy-start(f32[1,16,16384]{2,1,0:T(8,128)} %copy-done.4) | copy-start | bytes 3145732
  461.5 19.6 %copy-start.6 = (f32[1,16,16384]{2,1,0:T(8,128)S(1)}, f32[1,16,16384]{2,1,0:T(8,128)}, u32[]{:S(2)}) copy-start(f32[1,16,16384]{2,1,0:T(8,128)} %reshape.189) | copy-start | bytes 3145732
  464.0 8.3 %collective-permute-start.4 = (f32[1,1,4,16384]{3,2,0,1:T(4,128)S(1)}, f32[1,1,4,16384]{3,2,0,1:T(4,128)S(1)}, u32[]{:S(2)}, u32[]{:S(2)}) collective-permute-start(f32[1,1,4,16384]{3,2,0,1:T(4,128)S(1)} %get-tuple-element.6), channel_id=1, source_target_pairs={{0,32},{32,64},{64,96},{96,128},{128,160},{160,192},{192,224},{1,3... | collective-permute-start | bytes 786440 | tf_op jit(solution)/shard_map/ppermute | solution.py:17
  467.1 7.7 %collective-permute-start.5 = (f32[1,1,4,16384]{3,2,0,1:T(4,128)S(1)}, f32[1,1,4,16384]{3,2,0,1:T(4,128)S(1)}, u32[]{:S(2)}, u32[]{:S(2)}) collective-permute-start(f32[1,1,4,16384]{3,2,0,1:T(4,128)S(1)} %get-tuple-element.9), channel_id=1, source_target_pairs={{32,0},{64,32},{96,64},{128,96},{160,128},{192,160},{224,192},{33,... | collective-permute-start | bytes 786440 | tf_op jit(solution)/shard_map/ppermute | solution.py:19
  469.0 7.9 %collective-permute-start.6 = (f32[1,1,4,16384]{3,2,0,1:T(4,128)S(1)}, f32[1,1,4,16384]{3,2,0,1:T(4,128)S(1)}, u32[]{:S(2)}, u32[]{:S(2)}) collective-permute-start(f32[1,1,4,16384]{3,2,0,1:T(4,128)S(1)} %get-tuple-element.8), channel_id=1, source_target_pairs={{0,1},{1,2},{2,3},{3,4},{4,5},{5,6},{6,7},{7,8},{8,9},{9,10},{10,1... | collective-permute-start | bytes 786440 | tf_op jit(solution)/shard_map/ppermute | solution.py:17
  471.0 10.1 %collective-permute-start.7 = (f32[1,1,4,16384]{3,2,0,1:T(4,128)S(1)}, f32[1,1,4,16384]{3,2,0,1:T(4,128)S(1)}, u32[]{:S(2)}, u32[]{:S(2)}) collective-permute-start(f32[1,1,4,16384]{3,2,0,1:T(4,128)S(1)} %get-tuple-element.7), channel_id=1, source_target_pairs={{1,0},{2,1},{3,2},{4,3},{5,4},{6,5},{7,6},{8,7},{9,8},{10,9},{11,1... | collective-permute-start | bytes 786440 | tf_op jit(solution)/shard_map/ppermute | solution.py:19
Sparse Core Ops, SparseCore 0:
  12.7 211.5 reduce-scatter.1
